TPU v7x, 512 devices: a whole 4x4x16 slice. The times are simulated.
512 devices in a mesh: lon: 8 (over y, core), lat: 16 (over z), depth: 4 (over x).
Axes of the slice: x: 4, y: 4, z: 16, core: 2. Of those that a mesh axis runs over, the one named last changes fastest.
Arguments:
- snapshots: float32 [524288, 256], P(('lon', 'lat', 'depth')), may hold values from -300 to 300
- live_rows: int32 [512], P(('lon', 'lat', 'depth')), may hold values from 128 to 1024, as said below
- column_order: int32 [256], replicated, may hold values from 0 to 255, each once
Outputs:
- snapshot_basis: float32 [524288, 256], P(('lon', 'lat', 'depth'))
- triangular: float32 [256, 256], replicated
- highpass: float32 [524288, 256], P(('lon', 'lat', 'depth'))
Inputs may be any that keep to these rules, and one draw needn't show every extreme that they name: `live_rows`: each entry is a multiple of 128; some block has all 1024 rows live and some other block has 128.
All inputs are finite; a program needn't handle non-finite values.
Results may differ from a plain program's by a relative error of at most 0.00005.
Values sent between devices are 32-bit elements; how exact they have to be, the bound alone decides.
A program may use at most 64 MiB of HBM per device.

v0:
```python
import jax
import jax.numpy as jnp
from jax import lax
from jax.sharding import PartitionSpec as P

LOW = 32


def on_device(snapshots, live_rows, column_order):
    row_count = snapshots.shape[0]
    total_rows = row_count * lax.axis_size("lon") * lax.axis_size("lat") * lax.axis_size("depth")
    picked = jnp.take(snapshots, column_order, axis=1)
    live_mask = (lax.iota(jnp.int32, row_count) < live_rows[0])[:, None]
    masked = jnp.where(live_mask, picked, jnp.zeros_like(picked))
    local_gram = (
        lax.dot_general(masked, masked, (((0,), (0,)), ((), ())), precision=lax.Precision.HIGHEST)
        / total_rows
    )
    global_gram = lax.psum(local_gram, ("lon", "lat", "depth"))
    lower_factor = jnp.linalg.cholesky(global_gram)
    triangular = lower_factor.T
    snapshot_basis = jax.scipy.linalg.solve_triangular(lower_factor, masked.T, lower=True).T
    highpass = masked - jnp.dot(
        snapshot_basis[:, :LOW], triangular[:LOW, :], precision=lax.Precision.HIGHEST
    )
    return (snapshot_basis, triangular, highpass)


def solution(mesh):
    placed = (P(("lon", "lat", "depth"), None), P(("lon", "lat", "depth")), P())
    return jax.shard_map(
        on_device,
        mesh=mesh,
        in_specs=placed,
        out_specs=(P(("lon", "lat", "depth"), None), P(), P(("lon", "lat", "depth"), None)),
        check_vma=False,
    )
```

profile of v0, /device:TPU:1, one launch (start us, length us, event | category | flops | bytes accessed | tf_op | source)
XLA Modules:
  0.0 558.8 jit_solution(3424189647287764068)
XLA Ops:
  7.2 0.7 compare_select_fusion
  7.9 1.6 copy.6
  9.5 1.1 gather_fusion
  10.6 0.3 copy.7
  11.8 2.5 convolution_multiply_fusion
  14.4 469.9 %all-reduce.3.cloned.1.call-done = f32[256,256]{0,1:T(8,128)} async-done(((f32[256,256]{0,1:T(8,128)}), f32[256,256]{0,1:T(8,128)}) %all-reduce.3.cloned.1.call-update) | async-done | bytes 262160 | tf_op jit(solution)/shard_map/psum | solution.py:19
  484.2 1.1 copy.9
  485.5 11.7 %cholesky.50 = f32[128,128]{1,0:T(8,128)S(1)} custom-call(f32[128,128]{1,0:T(8,128)S(1)} %cholesky.118), custom_call_target="Cholesky" | custom-call | tf_op jit(solution)/shard_map/jit(cholesky)/cholesky | solution.py:20
  497.2 9.8 %custom-call.15 = f32[1,128,128]{1,2,0:T(8,128)S(1)} custom-call(f32[1,128,128]{2,1,0:T(8,128)S(1)} %get-tuple-element.29), custom_call_target="InvertDiagBlocksLowerTriangular" | custom-call | tf_op jit(solution)/shard_map/jit(cholesky)/cholesky | solution.py:20
  507.4 0.3 convolution_subtract_fusion.2
  507.7 11.9 %cholesky.105 = f32[128,128]{1,0:T(8,128)S(1)} custom-call(f32[128,128]{1,0:T(8,128)S(1)} %convolution_subtract_fusion.2), custom_call_target="Cholesky" | custom-call | tf_op jit(solution)/shard_map/jit(cholesky)/cholesky | solution.py:20
  519.7 0.6 compare_reduce_fusion
  521.7 4.0 while.1
  521.7 0.6 fusion.20
  522.3 1.4 bitcast_dynamic-update-slice_fusion.2
  523.7 0.6 fusion.20
  524.3 1.4 bitcast_dynamic-update-slice_fusion.2
  525.7 19.7 %custom-call.16 = f32[2,128,128]{1,2,0:T(8,128)S(1)} custom-call(f32[2,128,128]{2,1,0:T(8,128)S(1)} %get-tuple-element.10), custom_call_target="InvertDiagBlocksLowerTriangular" | custom-call | tf_op jit(solution)/shard_map/jit(_solve_triangular)/triangular_solve | solution.py:22
  545.4 0.6 fusion
  546.0 1.0 convolution_subtract_fusion.1
  547.0 0.6 fusion.8
  547.8 1.3 copy.11
  549.1 2.0 convolution_subtract_fusion
  551.1 0.8 copy.12
  (25 shorter events, 1.0 us)
Async XLA Ops:
  7.2 0.8 copy-start.1
  7.2 477.1 %all-reduce.3.cloned.1.call-start = ((), (), s32[]{:S(2)}) async-start(), calls=%async_computation | async-start | bytes 524288 | tf_op jit(solution)/shard_map/psum | solution.py:19
  484.2 1.2 copy-start
Sparse Core Ops, SparseCore 0:
  14.5 469.7 all-reduce.2
where the time goes:
time: 559 us
  waiting for transfers between devices  470 us (84%)
  other arithmetic  54.9 us (10%)
  between operations  16.2 us (3%)
  local copies, waits for them, and re-layouts  10.4 us (2%)
  matrix products  7.37 us (1%)
    psum x1, waiting for transfers between devices, on_device(): global_gram = lax.psum(local_gram, ('lon', 'lat', 'depth'))  470 us
    another operation x6, other arithmetic, on_device(): lower_factor = jnp.linalg.cholesky(global_gram)  34.1 us
    another operation x2, other arithmetic, on_device(): jax.scipy.linalg.solve_triangular(lower_factor, masked.T, lower=True)  19.7 us
  transfers between devices with their start and end apart: 1, of which 1 were waited for; matrix products, arithmetic and copies ran while one was open for 0% of the time, Pallas kernels for 0%

commit v1 on v0

v1 whole, which is shorter than its diff:
```python
import functools

import jax
import jax.numpy as jnp
from jax import lax
from jax.experimental import pallas as pl
from jax.experimental.pallas import tpu as pltpu
from jax.sharding import PartitionSpec as P

LOW = 32
CORES = 2
HIGHEST = lax.Precision.HIGHEST


def gram_kernel(total_rows, ny, nz, nx, snap_hbm, live_ref, order_ref, masked_ref, out_ref,
                snap, gram, half, from_core, from_y, quarter, from_x, strip, from_z,
                load_sem, send_sem, recv_sem):
    rows, width = snap.shape
    lon = lax.axis_index("lon")
    core, y = lax.rem(lon, CORES), lax.div(lon, CORES)
    z, x = lax.axis_index("lat"), lax.axis_index("depth")

    def at_core(c):
        return {"lon": y * CORES + c}

    def at_y(t):
        return {"lon": t * CORES + core}

    def at_z(t):
        return {"lat": t}

    def at_x(t):
        return {"depth": t}

    peers = [at_core(1 - core)]
    for d in range(1, ny):
        peers.append(at_y(lax.rem(y + d, ny)))
    for d in range(1, nx):
        peers.append(at_x(lax.rem(x + d, nx)))
    for d in range(1, nz):
        peers.append(at_z(lax.rem(z + d, nz)))

    barrier = pltpu.get_barrier_semaphore()
    for peer in peers:
        pl.semaphore_signal(barrier, inc=1, device_id=peer, device_id_type=pl.DeviceIdType.MESH)

    load = pltpu.make_async_copy(snap_hbm, snap, load_sem)
    load.start()
    select = (lax.broadcasted_iota(jnp.int32, (width, width), 0) == order_ref[...]).astype(jnp.bfloat16)
    load.wait()

    live = lax.broadcasted_iota(jnp.int32, (rows, width), 0) < live_ref[0]
    whole = jnp.where(live, snap[...], 0.0)
    high = whole.astype(jnp.bfloat16)
    rest = whole - high.astype(jnp.float32)
    middle = rest.astype(jnp.bfloat16)
    low = (rest - middle.astype(jnp.float32)).astype(jnp.bfloat16)
    masked = jnp.dot(high, select, preferred_element_type=jnp.float32)
    masked += jnp.dot(middle, select, preferred_element_type=jnp.float32)
    masked += jnp.dot(low, select, preferred_element_type=jnp.float32)
    masked_ref[...] = masked
    gram[...] = lax.dot_general(
        masked, masked, (((0,), (0,)), ((), ())), precision=HIGHEST, preferred_element_type=jnp.float32
    ) * (1.0 / total_rows)

    pl.semaphore_wait(barrier, len(peers))

    used = [0]

    def send(src, dst, peer):
        k = used[0]
        used[0] += 1
        copy = pltpu.make_async_remote_copy(
            src_ref=src, dst_ref=dst, send_sem=send_sem.at[k], recv_sem=recv_sem.at[k],
            device_id=peer, device_id_type=pl.DeviceIdType.MESH,
        )
        copy.start()
        return copy

    def part(ref, index, size):
        return ref.at[pl.ds(pl.multiple_of(index * size, size), size)]

    n_half = width // CORES
    n_quarter = n_half // ny
    n_strip = n_quarter // nx

    copy = send(part(gram, 1 - core, n_half), from_core, at_core(1 - core))
    copy.wait()
    half[...] = gram[pl.ds(pl.multiple_of(core * n_half, n_half), n_half), :] + from_core[...]

    def scatter(src, size, slots, n, me, at):
        copies = []
        for d in range(1, n):
            t = lax.rem(me + d, n)
            copies.append(send(part(src, t, size), slots.at[me], at(t)))
        slots[me] = src[pl.ds(pl.multiple_of(me * size, size), size), :]
        for copy in copies:
            copy.wait()
        total = slots[0]
        for s in range(1, n):
            total = total + slots[s]
        return total

    quarter[...] = scatter(half, n_quarter, from_y, ny, y, at_y)
    strip[...] = scatter(quarter, n_strip, from_x, nx, x, at_x)

    copies = []
    for d in range(1, nz):
        copies.append(send(strip, from_z.at[z], at_z(lax.rem(z + d, nz))))
    from_z[z] = strip[...]
    for copy in copies:
        copy.wait()
    total = from_z[0]
    for s in range(1, nz):
        total = total + from_z[s]
    place = core * (ny * nx) + y * nx + x
    out_ref[pl.ds(pl.multiple_of(place * n_strip, n_strip), n_strip), :] = total

    def gather(index, size, n, me, at):
        copies = []
        for d in range(1, n):
            copies.append(send(part(out_ref, index, size), part(out_ref, index, size), at(lax.rem(me + d, n))))
        for copy in copies:
            copy.wait()

    gather(place, n_strip, nx, x, at_x)
    gather(core * ny + y, n_quarter, ny, y, at_y)
    gather(core, n_half, CORES, core, at_core)


def masked_and_gram(snapshots, live_rows, column_order, sizes):
    rows, width = snapshots.shape
    ny, nz, nx = sizes
    n_half = width // CORES
    n_quarter = n_half // ny
    n_strip = n_quarter // nx
    copies = 2 + 2 * (ny - 1) + 2 * (nx - 1) + (nz - 1)
    total_rows = rows * CORES * ny * nz * nx
    f32 = jnp.float32
    return pl.pallas_call(
        functools.partial(gram_kernel, total_rows, ny, nz, nx),
        out_shape=(
            jax.ShapeDtypeStruct((rows, width), f32),
            jax.ShapeDtypeStruct((width, width), f32),
        ),
        in_specs=[
            pl.BlockSpec(memory_space=pl.ANY),
            pl.BlockSpec(memory_space=pltpu.SMEM),
            pl.BlockSpec(memory_space=pltpu.VMEM),
        ],
        out_specs=(pl.BlockSpec(memory_space=pltpu.VMEM), pl.BlockSpec(memory_space=pltpu.VMEM)),
        scratch_shapes=[
            pltpu.VMEM((rows, width), f32),
            pltpu.VMEM((width, width), f32),
            pltpu.VMEM((n_half, width), f32),
            pltpu.VMEM((n_half, width), f32),
            pltpu.VMEM((ny, n_quarter, width), f32),
            pltpu.VMEM((n_quarter, width), f32),
            pltpu.VMEM((nx, n_strip, width), f32),
            pltpu.VMEM((n_strip, width), f32),
            pltpu.VMEM((nz, n_strip, width), f32),
            pltpu.SemaphoreType.DMA,
            pltpu.SemaphoreType.DMA((copies,)),
            pltpu.SemaphoreType.DMA((copies,)),
        ],
        compiler_params=pltpu.CompilerParams(collective_id=0, has_side_effects=True),
        name="gram_allreduce",
    )(snapshots, live_rows, column_order.reshape(1, width))


def on_device(sizes, snapshots, live_rows, column_order):
    masked, global_gram = masked_and_gram(snapshots, live_rows, column_order, sizes)
    lower_factor = jnp.linalg.cholesky(global_gram)
    triangular = lower_factor.T
    snapshot_basis = jax.scipy.linalg.solve_triangular(lower_factor, masked.T, lower=True).T
    highpass = masked - jnp.dot(
        snapshot_basis[:, :LOW], triangular[:LOW, :], precision=lax.Precision.HIGHEST
    )
    return (snapshot_basis, triangular, highpass)


def solution(mesh):
    placed = (P(("lon", "lat", "depth"), None), P(("lon", "lat", "depth")), P())
    sizes = (mesh.shape["lon"] // CORES, mesh.shape["lat"], mesh.shape["depth"])
    return jax.shard_map(
        functools.partial(on_device, sizes),
        mesh=mesh,
        in_specs=placed,
        out_specs=(P(("lon", "lat", "depth"), None), P(), P(("lon", "lat", "depth"), None)),
        check_vma=False,
    )
```

time: 559 us -> 114 us (0.20)
  waiting for transfers between devices: 470 us -> 0 us
  Pallas kernels: 0 us -> 44.8 us
  between operations: 16.2 us -> 2.76 us
    psum x1 -> x0, waiting for transfers between devices: 470 us -> none  [on_device(): global_gram = lax.psum(local_gram, ('lon', 'lat', 'depth'))]
    pallas_call x0 -> x1, Pallas kernels: none -> 44.8 us  [masked_and_gram(): pl.pallas_call(functools.partial(gram_kernel, total_rows, ny, nz, nx), ou...]
  transfers between devices with their start and end apart: 1 -> 0, of which waited for: 1 -> 0; matrix products, arithmetic and copies ran while one was open for 0% -> 0% of each run, Pallas kernels for 0% -> 0%
where the time goes in v1:
time: 114 us
  other arithmetic  53.9 us (47%)
  Pallas kernels  44.8 us (39%)
  local copies, waits for them, and re-layouts  7.44 us (7%)
  matrix products  4.85 us (4%)
  between operations  2.76 us (2%)
    pallas_call x1, Pallas kernels, masked_and_gram(): pl.pallas_call(functools.partial(gram_kernel, total_rows, ny, nz, nx), ou...  44.8 us
    another operation x6, other arithmetic, on_device(): lower_factor = jnp.linalg.cholesky(global_gram)  34.1 us
    another operation x2, other arithmetic, on_device(): jax.scipy.linalg.solve_triangular(lower_factor, masked.T, lower=True)  19.7 us
    another operation x6, local copies, waits for them, and re-layouts  3.95 us

profile of v1, /device:TPU:1, one launch (start us, length us, event | category | flops | bytes accessed | tf_op | source)
XLA Modules:
  0.0 113.9 jit_solution(15273019755653441827)
XLA Ops:
  1.3 44.8 %gram_allreduce.1 = (f32[1024,256]{1,0:T(8,128)}, f32[256,256]{1,0:T(8,128)}) custom-call(f32[1024,256]{1,0:T(8,128)} %snap_hbm.1, s32[1]{0:T(128)S(6)} %copy.20.live_ref, s32[1,256]{1,0:T(1,128)} %bitcast.37), custom_call_target="tpu_custom_call" | custom-call | tf_op jit(solution)/shard_map/gram_allreduce/pallas_call | solution.py:140
  46.1 1.1 %copy.6 = f32[256,256]{0,1:T(8,128)S(1)} copy(f32[256,256]{1,0:T(8,128)} %get-tuple-element.5) | data formatting | bytes 524288 | tf_op jit(solution)/shard_map/gram_allreduce/pallas_call | solution.py:140
  47.4 11.7 %cholesky.50 = f32[128,128]{1,0:T(8,128)S(1)} custom-call(f32[128,128]{1,0:T(8,128)S(1)} %cholesky.118), custom_call_target="Cholesky" | custom-call | tf_op jit(solution)/shard_map/jit(cholesky)/cholesky | solution.py:173
  59.1 9.8 %custom-call.15 = f32[1,128,128]{1,2,0:T(8,128)S(1)} custom-call(f32[1,128,128]{2,1,0:T(8,128)S(1)} %get-tuple-element.33), custom_call_target="InvertDiagBlocksLowerTriangular" | custom-call | tf_op jit(solution)/shard_map/jit(cholesky)/cholesky | solution.py:173
  68.9 0.3 fusion.9
  69.2 0.1 copy.7
  69.4 0.3 convolution_subtract_fusion.2
  69.7 11.8 %cholesky.105 = f32[128,128]{1,0:T(8,128)S(1)} custom-call(f32[128,128]{1,0:T(8,128)S(1)} %convolution_subtract_fusion.2), custom_call_target="Cholesky" | custom-call | tf_op jit(solution)/shard_map/jit(cholesky)/cholesky | solution.py:173
  81.5 0.6 compare_reduce_fusion
  83.5 0.1 triangular_solve.57
  83.6 4.0 %while.1 = (s32[]{:T(128)}, f32[256,256]{1,0:T(8,128)S(1)}, s32[2,2]{1,0:T(2,128)S(1)}, f32[2,128,128]{2,1,0:T(8,128)S(1)}, s32[]{:T(128)}) while((s32[]{:T(128)}, f32[256,256]{1,0:T(8,128)S(1)}, s32[2,2]{1,0:T(2,128)S(1)}, f32[2,128,128]{2,1,0:T(8,128)S(1)}, s32[]{:T(128)}) %tuple.28), condition=%wide.while_cond, body=%wide.while_body.sunk | while | flops 2 | bytes 131181 | solution.py:175
  83.6 0.6 fusion.18
  84.2 1.4 %bitcast_dynamic-update-slice_fusion.2 = f32[2,128,128]{2,1,0:T(8,128)S(1)} fusion(f32[2,128,128]{2,1,0:T(8,128)S(1)} %get-tuple-element.73, s32[]{:T(128)} %get-tuple-element.70, f32[256,256]{1,0:T(8,128)S(1)} %get-tuple-element.76, s32[]{:T(128)} %bitcast.33, s32[]{:T(128)} %bitcast.34), kind=kLoop, calls=%fused_computation.clone.1 | loop fusion | bytes 131084 | tf_op jit(solution)/shard_map/jit(_solve_triangular)/triangular_solve
  85.6 0.6 fusion.18
  86.2 1.4 %bitcast_dynamic-update-slice_fusion.2 = f32[2,128,128]{2,1,0:T(8,128)S(1)} fusion(f32[2,128,128]{2,1,0:T(8,128)S(1)} %get-tuple-element.73, s32[]{:T(128)} %get-tuple-element.70, f32[256,256]{1,0:T(8,128)S(1)} %get-tuple-element.76, s32[]{:T(128)} %bitcast.33, s32[]{:T(128)} %bitcast.34), kind=kLoop, calls=%fused_computation.clone.1 | loop fusion | bytes 131084 | tf_op jit(solution)/shard_map/jit(_solve_triangular)/triangular_solve
  87.6 19.7 %custom-call.16 = f32[2,128,128]{1,2,0:T(8,128)S(1)} custom-call(f32[2,128,128]{2,1,0:T(8,128)S(1)} %get-tuple-element.14), custom_call_target="InvertDiagBlocksLowerTriangular" | custom-call | tf_op jit(solution)/shard_map/jit(_solve_triangular)/triangular_solve | solution.py:175
  107.3 0.0 copy-done
  107.3 0.6 fusion
  107.9 1.0 convolution_subtract_fusion.1
  108.9 0.6 fusion.8
  109.6 0.1 maximum_bitcast_fusion
  109.7 2.0 %convolution_subtract_fusion = f32[1024,256]{1,0:T(8,128)} fusion(f32[1024,256]{1,0:T(8,128)S(1)} %copy-done, f32[256,256]{0,1:T(8,128)S(1)} %get-tuple-element.28, f32[1024,256]{0,1:T(8,128)S(1)} %maximum_bitcast_fusion), kind=kOutput, calls=%fused_computation.2 | convolution fusion | flops 100925440 | bytes 2359296 | tf_op jit(solution)/shard_map/dot_general | solution.py:176
  111.7 1.3 %copy.8 = f32[1024,256]{1,0:T(8,128)} copy(f32[1024,256]{0,1:T(8,128)S(1)} %maximum_bitcast_fusion) | data formatting | bytes 2097152
  113.0 0.8 copy.9
  (14 shorter events, 0.2 us)
Async XLA Ops:
  46.1 1.2 %copy-start.1 = (f32[256,256]{1,0:T(8,128)S(1)}, f32[256,256]{1,0:T(8,128)}, u32[]{:S(2)}) copy-start(f32[256,256]{1,0:T(8,128)} %get-tuple-element.5) | copy-start | bytes 786436
  69.4 37.9 %copy-start = (f32[1024,256]{1,0:T(8,128)S(1)}, f32[1024,256]{1,0:T(8,128)}, u32[]{:S(2)}) copy-start(f32[1024,256]{1,0:T(8,128)} %get-tuple-element.6) | copy-start | bytes 3145732

commit v2 on v1

--- a/solution.py
+++ b/solution.py
@@ -9,6 +9,8 @@
 
 LOW = 32
 CORES = 2
+LANES = 128
+TILE = 8
 HIGHEST = lax.Precision.HIGHEST
 
 
@@ -168,15 +170,145 @@
     )(snapshots, live_rows, column_order.reshape(1, width))
 
 
+def factor_kernel(group, gram_ref, masked_ref, basis_ref, tri_ref, high_ref, work, inverse):
+    width = gram_ref.shape[0]
+    rows = masked_ref.shape[0]
+    blocks = width // TILE
+    per_lanes = LANES // TILE
+    f32 = jnp.float32
+    shape = (TILE, LANES)
+    sub = lax.broadcasted_iota(jnp.int32, shape, 0)
+    lane = lax.broadcasted_iota(jnp.int32, shape, 1)
+
+    def band(i):
+        return slice(i * TILE, (i + 1) * TILE)
+
+    def lanes(v):
+        return slice(v * LANES, (v + 1) * LANES)
+
+    work[...] = gram_ref[...]
+    row_id = lax.broadcasted_iota(jnp.int32, (width, width), 0)
+    col_id = lax.broadcasted_iota(jnp.int32, (width, width), 1)
+    inverse[...] = (row_id == col_id).astype(f32)
+    tri_ref[...] = jnp.zeros_like(tri_ref)
+
+    chunk = 128
+
+    def finish_high(c):
+        here = slice(c * chunk, (c + 1) * chunk)
+        a = masked_ref[here, :]
+        q = lax.dot_general(a, inverse[:LOW, :], (((1,), (1,)), ((), ())), precision=HIGHEST,
+                            preferred_element_type=f32)
+        high_ref[here, :] = a - jnp.dot(q, tri_ref[:LOW, :], precision=HIGHEST, preferred_element_type=f32)
+
+    def finish_basis(c, half):
+        here = slice(c * chunk, (c + 1) * chunk)
+        depth = (half + 1) * LANES
+        basis_ref[here, lanes(half)] = lax.dot_general(
+            masked_ref[here, :depth], inverse[lanes(half), :depth], (((1,), (1,)), ((), ())),
+            precision=HIGHEST, preferred_element_type=f32)
+
+    fillers = []
+
+    for k in range(blocks):
+        t = k // per_lanes
+        base = (k % per_lanes) * TILE
+        last = (k // group + 1) * group
+        row = {}
+        for j in range(TILE):
+            r = k * TILE + j
+            for v in range(t, width // LANES):
+                row["g", v, j] = jnp.broadcast_to(work[r:r + 1, lanes(v)], shape)
+            for v in range(0, t + 1):
+                row["x", v, j] = jnp.broadcast_to(inverse[r:r + 1, lanes(v)], shape)
+        items = [("g", v) for v in range(t, width // LANES)] + [("x", v) for v in range(0, t + 1)]
+        a = {}
+        for j in range(TILE):
+            for m in range(j, TILE):
+                a[j, m] = jnp.broadcast_to(row["g", t, j][:, base + m:base + m + 1], shape)
+        col = {}
+        for i in range(k + 1, last):
+            tile = work[band(i), lanes(t)]
+            for j in range(TILE):
+                col[i, j] = jnp.broadcast_to(tile[:, base + j:base + j + 1], shape)
+        for j in range(TILE):
+            s = lax.rsqrt(a[j, j])
+            for m in range(j + 1, TILE):
+                a[j, m] = a[j, m] * s
+            for m in range(j + 1, TILE):
+                for p in range(m, TILE):
+                    a[m, p] = a[m, p] - a[j, m] * a[j, p]
+            for i in range(k + 1, last):
+                col[i, j] = col[i, j] * s
+                for m in range(j + 1, TILE):
+                    col[i, m] = col[i, m] - a[j, m] * col[i, j]
+            for kind, v in items:
+                row[kind, v, j] = row[kind, v, j] * s
+                for m in range(j + 1, TILE):
+                    row[kind, v, m] = row[kind, v, m] - a[j, m] * row[kind, v, j]
+        for i in range(k + 1, last):
+            for kind, v in items:
+                ref = work if kind == "g" else inverse
+                change = [col[i, j] * row[kind, v, j] for j in range(TILE)]
+                while len(change) > 1:
+                    change = [p + q for p, q in zip(change[::2], change[1::2])]
+                ref[band(i), lanes(v)] = ref[band(i), lanes(v)] - change[0]
+        for kind, v in items:
+            tile = row[kind, v, TILE - 1]
+            for j in range(TILE - 2, -1, -1):
+                tile = jnp.where(sub == j, row[kind, v, j], tile)
+            if kind == "g":
+                if v == t:
+                    tile = jnp.where(lane >= sub + base, tile, 0.0)
+                tri_ref[band(k), lanes(v)] = tile
+            else:
+                inverse[band(k), lanes(v)] = tile
+
+        if k + 1 == last and last < blocks:
+            first = last - group
+            done = slice(first * TILE, last * TILE)
+            low = (last // per_lanes) * LANES
+            span = (t + 1) * LANES
+            left = tri_ref[done, low:]
+            dims = (((0,), (0,)), ((), ()))
+            drop = lax.dot_general(left, tri_ref[done, low:], dims, precision=HIGHEST, preferred_element_type=f32)
+            fill = lax.dot_general(left, inverse[done, :span], dims, precision=HIGHEST, preferred_element_type=f32)
+            skip = last * TILE - low
+            work[last * TILE:, low:] = work[last * TILE:, low:] - drop[skip:, :]
+            inverse[last * TILE:, :span] = inverse[last * TILE:, :span] - fill[skip:, :]
+        if (k + 1) * TILE == LOW:
+            fillers += [functools.partial(finish_high, c) for c in range(rows // chunk)]
+        if (k + 1) * TILE == LANES:
+            fillers += [functools.partial(finish_basis, c, 0) for c in range(rows // chunk)]
+        if fillers:
+            fillers.pop(0)()
+    for c in range(rows // chunk):
+        fillers.append(functools.partial(finish_basis, c, 1))
+    for filler in fillers:
+        filler()
+
+
+def factor(gram, masked, group=4):
+    rows, width = masked.shape
+    f32 = jnp.float32
+    vmem = pl.BlockSpec(memory_space=pltpu.VMEM)
+    return pl.pallas_call(
+        functools.partial(factor_kernel, group),
+        out_shape=(
+            jax.ShapeDtypeStruct((rows, width), f32),
+            jax.ShapeDtypeStruct((width, width), f32),
+            jax.ShapeDtypeStruct((rows, width), f32),
+        ),
+        in_specs=[vmem, vmem],
+        out_specs=(vmem, vmem, vmem),
+        scratch_shapes=[pltpu.VMEM((width, width), f32), pltpu.VMEM((width, width), f32)],
+        name="factor",
+    )(gram, masked)
+
+
 def on_device(sizes, snapshots, live_rows, column_order):
     masked, global_gram = masked_and_gram(snapshots, live_rows, column_order, sizes)
-    lower_factor = jnp.linalg.cholesky(global_gram)
-    triangular = lower_factor.T
-    snapshot_basis = jax.scipy.linalg.solve_triangular(lower_factor, masked.T, lower=True).T
-    highpass = masked - jnp.dot(
-        snapshot_basis[:, :LOW], triangular[:LOW, :], precision=lax.Precision.HIGHEST
-    )
-    return (snapshot_basis, triangular, highpass)
+    return factor(global_gram, masked)
 
 
 def solution(mesh):

time: 114 us -> 57.9 us (0.51)
  other arithmetic: 53.9 us -> 0 us
  Pallas kernels: 44.8 us -> 56.4 us
  local copies, waits for them, and re-layouts: 7.44 us -> 0 us
  matrix products: 4.85 us -> 0 us
  between operations: 2.76 us -> 1.28 us
    another operation x8 -> x0, other arithmetic: 53.8 us -> none  [the longest x6 34.1 us: on_device(): lower_factor = jnp.linalg.cholesky(global_gram)]
    pallas_call x0 -> x1, Pallas kernels: none -> 11.5 us  [factor(): pl.pallas_call(functools.partial(factor_kernel, group), out_shape=(jax.Sh...]
    another operation x11 -> x0, local copies, waits for them, and re-layouts: 4.15 us -> none
    another operation x5 -> x0, matrix products: 2.85 us -> none  [the longest x3 2.27 us: on_device(): jax.scipy.linalg.solve_triangular(lower_factor, masked.T, lower=True)]
    unnamed x6 -> x0, local copies, waits for them, and re-layouts: 2.15 us -> none
    dot_general x1 -> x0, matrix products: 2 us -> none  [on_device(): jnp.dot(snapshot_basis[:, :LOW], triangular[:LOW, :], precision=lax.Preci...]
    pallas_call x1 -> x0, local copies, waits for them, and re-layouts: 1.14 us -> none  [masked_and_gram(): pl.pallas_call(functools.partial(gram_kernel, total_rows, ny, nz, nx), ou...]
where the time goes in v2:
time: 57.9 us; the launch traced here: 57.7 us
  Pallas kernels  56.4 us (97%)
  between operations  1.28 us (2%)
    pallas_call x1, Pallas kernels, masked_and_gram(): pl.pallas_call(functools.partial(gram_kernel, total_rows, ny, nz, nx), ou...  44.9 us
    pallas_call x1, Pallas kernels, factor(): pl.pallas_call(functools.partial(factor_kernel, group), out_shape=(jax.Sh...  11.5 us

profile of v2, /device:TPU:1, one launch (start us, length us, event | category | flops | bytes accessed | tf_op | source)
XLA Modules:
  0.0 57.7 jit_solution(5681510124611630291)
XLA Ops:
  1.3 44.9 %gram_allreduce.1 = (f32[1024,256]{1,0:T(8,128)}, f32[256,256]{1,0:T(8,128)}) custom-call(f32[1024,256]{1,0:T(8,128)} %snap_hbm.1, s32[1]{0:T(128)S(6)} %copy.6.live_ref, s32[1,256]{1,0:T(1,128)} %bitcast.1), custom_call_target="tpu_custom_call" | custom-call | tf_op jit(solution)/shard_map/gram_allreduce/pallas_call | solution.py:142
  46.1 11.5 %factor.1 = (f32[1024,256]{1,0:T(8,128)}, f32[256,256]{1,0:T(8,128)}, f32[1024,256]{1,0:T(8,128)}) custom-call(f32[256,256]{1,0:T(8,128)} %get-tuple-element.5.gram_ref, f32[1024,256]{1,0:T(8,128)} %get-tuple-element.6.masked_ref), custom_call_target="tpu_custom_call" | custom-call | tf_op jit(solution)/shard_map/factor/pallas_call | solution.py:295

commit v3 on v2

--- a/solution.py
+++ b/solution.py
@@ -11,37 +11,41 @@
 CORES = 2
 LANES = 128
 TILE = 8
+UNIT = 4
 HIGHEST = lax.Precision.HIGHEST
 
 
-def gram_kernel(total_rows, ny, nz, nx, snap_hbm, live_ref, order_ref, masked_ref, out_ref,
-                snap, gram, half, from_core, from_y, quarter, from_x, strip, from_z,
-                load_sem, send_sem, recv_sem):
+def hops(d, n):
+    return min(d % n, n - d % n)
+
+
+def gram_kernel(total_rows, ny, nz, nx, snap_hbm, live_ref, order_ref, masked_hbm, out_ref,
+                snap, masked_ref, gram, from_core, half, from_plane, strip, from_z,
+                load_sem, store_sem, send_sem, recv_sem):
     rows, width = snap.shape
     lon = lax.axis_index("lon")
     core, y = lax.rem(lon, CORES), lax.div(lon, CORES)
     z, x = lax.axis_index("lat"), lax.axis_index("depth")
-
-    def at_core(c):
-        return {"lon": y * CORES + c}
-
-    def at_y(t):
-        return {"lon": t * CORES + core}
-
-    def at_z(t):
-        return {"lat": t}
-
-    def at_x(t):
-        return {"depth": t}
-
-    peers = [at_core(1 - core)]
-    for d in range(1, ny):
-        peers.append(at_y(lax.rem(y + d, ny)))
-    for d in range(1, nx):
-        peers.append(at_x(lax.rem(x + d, nx)))
-    for d in range(1, nz):
-        peers.append(at_z(lax.rem(z + d, nz)))
-
+    f32 = jnp.float32
+
+    plane = [(dy, dx) for dy in range(ny) for dx in range(nx) if dy or dx]
+    plane.sort(key=lambda d: -hops(d[0], ny) - hops(d[1], nx))
+    line = sorted(range(1, nz), key=lambda d: -hops(d, nz))
+
+    def other_core():
+        return {"lon": y * CORES + 1 - core}
+
+    def in_plane(dy, dx):
+        return lax.rem(y + dy, ny), lax.rem(x + dx, nx)
+
+    def at_plane(dy, dx):
+        ty, tx = in_plane(dy, dx)
+        return {"lon": ty * CORES + core, "depth": tx}
+
+    def at_z(d):
+        return {"lat": lax.rem(z + d, nz)}
+
+    peers = [at_z(d) for d in line] + [at_plane(*d) for d in plane] + [other_core()]
     barrier = pltpu.get_barrier_semaphore()
     for peer in peers:
         pl.semaphore_signal(barrier, inc=1, device_id=peer, device_id_type=pl.DeviceIdType.MESH)
@@ -54,16 +58,26 @@
     live = lax.broadcasted_iota(jnp.int32, (rows, width), 0) < live_ref[0]
     whole = jnp.where(live, snap[...], 0.0)
     high = whole.astype(jnp.bfloat16)
-    rest = whole - high.astype(jnp.float32)
+    rest = whole - high.astype(f32)
     middle = rest.astype(jnp.bfloat16)
-    low = (rest - middle.astype(jnp.float32)).astype(jnp.bfloat16)
-    masked = jnp.dot(high, select, preferred_element_type=jnp.float32)
-    masked += jnp.dot(middle, select, preferred_element_type=jnp.float32)
-    masked += jnp.dot(low, select, preferred_element_type=jnp.float32)
+    low = (rest - middle.astype(f32)).astype(jnp.bfloat16)
+    masked = jnp.dot(high, select, preferred_element_type=f32)
+    masked += jnp.dot(middle, select, preferred_element_type=f32)
+    masked += jnp.dot(low, select, preferred_element_type=f32)
     masked_ref[...] = masked
-    gram[...] = lax.dot_general(
-        masked, masked, (((0,), (0,)), ((), ())), precision=HIGHEST, preferred_element_type=jnp.float32
-    ) * (1.0 / total_rows)
+    store = pltpu.make_async_copy(masked_ref, masked_hbm, store_sem)
+    store.start()
+
+    left, right = masked[:, :LANES], masked[:, LANES:]
+
+    def product(a, b, at):
+        block = lax.dot_general(a, b, (((0,), (0,)), ((), ())), precision=HIGHEST, preferred_element_type=f32)
+        gram[at * LANES // UNIT:(at + 1) * LANES // UNIT] = (block * (1.0 / total_rows)).reshape(
+            LANES // UNIT, UNIT, LANES)
+
+    product(left, left, 0)
+    product(left, right, 1)
+    product(right, right, 2)
 
     pl.semaphore_wait(barrier, len(peers))
 
@@ -79,88 +93,79 @@
         copy.start()
         return copy
 
-    def part(ref, index, size):
-        return ref.at[pl.ds(pl.multiple_of(index * size, size), size)]
-
-    n_half = width // CORES
-    n_quarter = n_half // ny
-    n_strip = n_quarter // nx
-
-    copy = send(part(gram, 1 - core, n_half), from_core, at_core(1 - core))
+    places = ny * nx
+    n_half = half.shape[0]
+    n_strip = n_half // places
+    place = y * nx + x
+
+    copy = send(gram.at[pl.ds((1 - core) * n_half, n_half)], from_core, other_core())
     copy.wait()
-    half[...] = gram[pl.ds(pl.multiple_of(core * n_half, n_half), n_half), :] + from_core[...]
-
-    def scatter(src, size, slots, n, me, at):
-        copies = []
-        for d in range(1, n):
-            t = lax.rem(me + d, n)
-            copies.append(send(part(src, t, size), slots.at[me], at(t)))
-        slots[me] = src[pl.ds(pl.multiple_of(me * size, size), size), :]
-        for copy in copies:
-            copy.wait()
-        total = slots[0]
-        for s in range(1, n):
-            total = total + slots[s]
-        return total
-
-    quarter[...] = scatter(half, n_quarter, from_y, ny, y, at_y)
-    strip[...] = scatter(quarter, n_strip, from_x, nx, x, at_x)
+    half[...] = gram[pl.ds(core * n_half, n_half)] + from_core[...]
 
     copies = []
-    for d in range(1, nz):
-        copies.append(send(strip, from_z.at[z], at_z(lax.rem(z + d, nz))))
+    for d in plane:
+        ty, tx = in_plane(*d)
+        copies.append(send(half.at[pl.ds((ty * nx + tx) * n_strip, n_strip)], from_plane.at[place], at_plane(*d)))
+    from_plane[place] = half[pl.ds(place * n_strip, n_strip)]
+    for copy in copies:
+        copy.wait()
+    total = from_plane[0]
+    for s in range(1, places):
+        total = total + from_plane[s]
+    strip[...] = total
+
+    copies = [send(strip, from_z.at[z], at_z(d)) for d in line]
     from_z[z] = strip[...]
     for copy in copies:
         copy.wait()
     total = from_z[0]
     for s in range(1, nz):
         total = total + from_z[s]
-    place = core * (ny * nx) + y * nx + x
-    out_ref[pl.ds(pl.multiple_of(place * n_strip, n_strip), n_strip), :] = total
-
-    def gather(index, size, n, me, at):
-        copies = []
-        for d in range(1, n):
-            copies.append(send(part(out_ref, index, size), part(out_ref, index, size), at(lax.rem(me + d, n))))
-        for copy in copies:
-            copy.wait()
-
-    gather(place, n_strip, nx, x, at_x)
-    gather(core * ny + y, n_quarter, ny, y, at_y)
-    gather(core, n_half, CORES, core, at_core)
+    mine = pl.ds((core * places + place) * n_strip, n_strip)
+    out_ref[mine] = total
+
+    copies = [send(out_ref.at[mine], out_ref.at[mine], at_plane(*d)) for d in plane]
+    for copy in copies:
+        copy.wait()
+    mine = pl.ds(core * n_half, n_half)
+    copy = send(out_ref.at[mine], out_ref.at[mine], other_core())
+    copy.wait()
+    store.wait()
 
 
 def masked_and_gram(snapshots, live_rows, column_order, sizes):
     rows, width = snapshots.shape
     ny, nz, nx = sizes
-    n_half = width // CORES
-    n_quarter = n_half // ny
-    n_strip = n_quarter // nx
-    copies = 2 + 2 * (ny - 1) + 2 * (nx - 1) + (nz - 1)
-    total_rows = rows * CORES * ny * nz * nx
+    places = ny * nx
+    units = 3 * LANES // UNIT
+    n_half = units // CORES
+    n_strip = n_half // places
+    copies = 2 + 2 * (places - 1) + (nz - 1)
+    total_rows = rows * CORES * places * nz
     f32 = jnp.float32
-    return pl.pallas_call(
+    tile = (UNIT, LANES)
+    masked, gram = pl.pallas_call(
         functools.partial(gram_kernel, total_rows, ny, nz, nx),
         out_shape=(
             jax.ShapeDtypeStruct((rows, width), f32),
-            jax.ShapeDtypeStruct((width, width), f32),
+            jax.ShapeDtypeStruct((units, *tile), f32),
         ),
         in_specs=[
             pl.BlockSpec(memory_space=pl.ANY),
             pl.BlockSpec(memory_space=pltpu.SMEM),
             pl.BlockSpec(memory_space=pltpu.VMEM),
         ],
-        out_specs=(pl.BlockSpec(memory_space=pltpu.VMEM), pl.BlockSpec(memory_space=pltpu.VMEM)),
+        out_specs=(pl.BlockSpec(memory_space=pl.ANY), pl.BlockSpec(memory_space=pltpu.VMEM)),
         scratch_shapes=[
             pltpu.VMEM((rows, width), f32),
-            pltpu.VMEM((width, width), f32),
-            pltpu.VMEM((n_half, width), f32),
-            pltpu.VMEM((n_half, width), f32),
-            pltpu.VMEM((ny, n_quarter, width), f32),
-            pltpu.VMEM((n_quarter, width), f32),
-            pltpu.VMEM((nx, n_strip, width), f32),
-            pltpu.VMEM((n_strip, width), f32),
-            pltpu.VMEM((nz, n_strip, width), f32),
+            pltpu.VMEM((rows, width), f32),
+            pltpu.VMEM((units, *tile), f32),
+            pltpu.VMEM((n_half, *tile), f32),
+            pltpu.VMEM((n_half, *tile), f32),
+            pltpu.VMEM((places, n_strip, *tile), f32),
+            pltpu.VMEM((n_strip, *tile), f32),
+            pltpu.VMEM((nz, n_strip, *tile), f32),
+            pltpu.SemaphoreType.DMA,
             pltpu.SemaphoreType.DMA,
             pltpu.SemaphoreType.DMA((copies,)),
             pltpu.SemaphoreType.DMA((copies,)),
@@ -168,11 +173,11 @@
         compiler_params=pltpu.CompilerParams(collective_id=0, has_side_effects=True),
         name="gram_allreduce",
     )(snapshots, live_rows, column_order.reshape(1, width))
+    return masked, gram.reshape(3 * LANES, LANES)
 
 
 def factor_kernel(group, gram_ref, masked_ref, basis_ref, tri_ref, high_ref, work, inverse):
-    width = gram_ref.shape[0]
-    rows = masked_ref.shape[0]
+    rows, width = masked_ref.shape
     blocks = width // TILE
     per_lanes = LANES // TILE
     f32 = jnp.float32
@@ -186,7 +191,10 @@
     def lanes(v):
         return slice(v * LANES, (v + 1) * LANES)
 
-    work[...] = gram_ref[...]
+    work[:LANES, :LANES] = gram_ref[:LANES, :]
+    work[:LANES, LANES:] = gram_ref[LANES:2 * LANES, :]
+    work[LANES:, :LANES] = jnp.zeros((width - LANES, LANES), f32)
+    work[LANES:, LANES:] = gram_ref[2 * LANES:, :]
     row_id = lax.broadcasted_iota(jnp.int32, (width, width), 0)
     col_id = lax.broadcasted_iota(jnp.int32, (width, width), 1)
     inverse[...] = (row_id == col_id).astype(f32)

time: 57.9 us -> 50.4 us (0.87)
  Pallas kernels: 56.4 us -> 48.9 us
    pallas_call x1, Pallas kernels: 44.9 us -> 37.3 us  [masked_and_gram(): pl.pallas_call(functools.partial(gram_kernel, total_rows, ny, nz, nx), ou...]
where the time goes in v3:
time: 50.4 us; the launch traced here: 50.2 us
  Pallas kernels  48.9 us (97%)
  between operations  1.28 us (3%)
    pallas_call x1, Pallas kernels, masked_and_gram(): pl.pallas_call(functools.partial(gram_kernel, total_rows, ny, nz, nx), ou...  37.3 us
    pallas_call x1, Pallas kernels, factor(): pl.pallas_call(functools.partial(factor_kernel, group), out_shape=(jax.Sh...  11.6 us

profile of v3, /device:TPU:1, one launch (start us, length us, event | category | flops | bytes accessed | tf_op | source)
XLA Modules:
  0.0 50.2 jit_solution(3452154391871736922)
XLA Ops:
  1.3 37.3 %gram_allreduce.1 = (f32[1024,256]{1,0:T(8,128)}, f32[96,4,128]{2,1,0:T(4,128)}) custom-call(f32[1024,256]{1,0:T(8,128)} %snap_hbm.1, s32[1]{0:T(128)S(6)} %copy.6.live_ref, s32[1,256]{1,0:T(1,128)} %bitcast.3), custom_call_target="tpu_custom_call" | custom-call | tf_op jit(solution)/shard_map/gram_allreduce/pallas_call | solution.py:147
  38.6 11.6 %factor.1 = (f32[1024,256]{1,0:T(8,128)}, f32[256,256]{1,0:T(8,128)}, f32[1024,256]{1,0:T(8,128)}) custom-call(f32[384,128]{1,0:T(8,128)} %bitcast.2, f32[1024,256]{1,0:T(8,128)} %get-tuple-element.6.masked_ref), custom_call_target="tpu_custom_call" | custom-call | tf_op jit(solution)/shard_map/factor/pallas_call | solution.py:303

commit v4 on v3

v4 whole, which is shorter than its diff:
```python
import functools

import jax
import jax.numpy as jnp
from jax import lax
from jax.experimental import pallas as pl
from jax.experimental.pallas import tpu as pltpu
from jax.sharding import PartitionSpec as P

LOW = 32
CORES = 2
LANES = 128
TILE = 8
UNIT = 4
LOADS = 4
BF16 = jnp.bfloat16
TERMS = ((2, 0), (0, 2), (1, 1), (1, 0), (0, 1), (0, 0))
HIGHEST = lax.Precision.HIGHEST


def hops(d, n):
    return min(d % n, n - d % n)


def gram_kernel(total_rows, ny, nz, nx, snap_hbm, live_ref, order_ref, out_ref, high_hbm, middle_hbm, low_hbm,
                snap, high_ref, middle_ref, low_ref, gram, from_core, half, from_plane, strip, from_z,
                load_sem, store_sem, send_sem, recv_sem):
    rows, width = snap.shape
    lon = lax.axis_index("lon")
    core, y = lax.rem(lon, CORES), lax.div(lon, CORES)
    z, x = lax.axis_index("lat"), lax.axis_index("depth")
    f32 = jnp.float32
    data = (high_ref, middle_ref, low_ref)
    data_hbm = (high_hbm, middle_hbm, low_hbm)

    plane = [(dy, dx) for dy in range(ny) for dx in range(nx) if dy or dx]
    plane.sort(key=lambda d: -hops(d[0], ny) - hops(d[1], nx))
    line = sorted(range(1, nz), key=lambda d: -hops(d, nz))

    def other_core():
        return {"lon": y * CORES + 1 - core}

    def in_plane(dy, dx):
        return lax.rem(y + dy, ny), lax.rem(x + dx, nx)

    def at_plane(dy, dx):
        ty, tx = in_plane(dy, dx)
        return {"lon": ty * CORES + core, "depth": tx}

    def at_z(d):
        return {"lat": lax.rem(z + d, nz)}

    size = rows // LOADS
    loads = []
    for c in range(LOADS):
        here = pl.ds(c * size, size)
        load = pltpu.make_async_copy(snap_hbm.at[here], snap.at[here], load_sem.at[c])
        load.start()
        loads.append(load)

    peers = [at_z(d) for d in line] + [at_plane(*d) for d in plane] + [other_core()]
    barrier = pltpu.get_barrier_semaphore()
    for peer in peers:
        pl.semaphore_signal(barrier, inc=1, device_id=peer, device_id_type=pl.DeviceIdType.MESH)

    select = (lax.broadcasted_iota(jnp.int32, (width, width), 0) == order_ref[...]).astype(BF16)
    for c in range(LOADS):
        loads[c].wait()
        here = slice(c * size, (c + 1) * size)
        live = lax.broadcasted_iota(jnp.int32, (size, width), 0) + c * size < live_ref[0]
        for piece, ref in zip(pieces(jnp.where(live, snap[here, :], 0.0)), data):
            ref[here, :] = jnp.dot(piece, select, preferred_element_type=f32).astype(BF16)
    stores = []
    for p, (src, dst) in enumerate(zip(data, data_hbm)):
        store = pltpu.make_async_copy(src, dst, store_sem.at[p])
        store.start()
        stores.append(store)

    def inner(a, b):
        return lax.dot_general(a, b, (((0,), (0,)), ((), ())), preferred_element_type=f32)

    high, middle, low = (ref[...] for ref in data)
    cross = inner(high, low) + inner(high, middle)
    whole = (inner(middle, middle) + (cross + cross.T) + inner(high, high)) * (1.0 / total_rows)

    blocks = (whole[:LANES, :LANES], whole[:LANES, LANES:], whole[LANES:, LANES:])
    per_block = LANES // UNIT
    for at, block in enumerate(blocks):
        gram[at * per_block:(at + 1) * per_block] = block.reshape(per_block, UNIT, LANES)

    pl.semaphore_wait(barrier, len(peers))

    used = [0]

    def send(src, dst, peer):
        k = used[0]
        used[0] += 1
        copy = pltpu.make_async_remote_copy(
            src_ref=src, dst_ref=dst, send_sem=send_sem.at[k], recv_sem=recv_sem.at[k],
            device_id=peer, device_id_type=pl.DeviceIdType.MESH,
        )
        copy.start()
        return copy

    places = ny * nx
    n_half = half.shape[0]
    n_strip = n_half // places
    place = y * nx + x

    copy = send(gram.at[pl.ds((1 - core) * n_half, n_half)], from_core, other_core())
    copy.wait()
    half[...] = gram[pl.ds(core * n_half, n_half)] + from_core[...]

    copies = []
    for d in plane:
        ty, tx = in_plane(*d)
        copies.append(send(half.at[pl.ds((ty * nx + tx) * n_strip, n_strip)], from_plane.at[place], at_plane(*d)))
    from_plane[place] = half[pl.ds(place * n_strip, n_strip)]
    for copy in copies:
        copy.wait()
    total = from_plane[0]
    for s in range(1, places):
        total = total + from_plane[s]
    strip[...] = total

    copies = [send(strip, from_z.at[z], at_z(d)) for d in line]
    from_z[z] = strip[...]
    for copy in copies:
        copy.wait()
    total = from_z[0]
    for s in range(1, nz):
        total = total + from_z[s]
    mine = pl.ds((core * places + place) * n_strip, n_strip)
    out_ref[mine] = total

    copies = [send(out_ref.at[mine], out_ref.at[mine], at_plane(*d)) for d in plane]
    for copy in copies:
        copy.wait()
    mine = pl.ds(core * n_half, n_half)
    copy = send(out_ref.at[mine], out_ref.at[mine], other_core())
    copy.wait()
    for store in stores:
        store.wait()


def masked_and_gram(snapshots, live_rows, column_order, sizes):
    rows, width = snapshots.shape
    ny, nz, nx = sizes
    places = ny * nx
    units = 3 * LANES // UNIT
    n_half = units // CORES
    n_strip = n_half // places
    copies = 2 + 2 * (places - 1) + (nz - 1)
    total_rows = rows * CORES * places * nz
    f32 = jnp.float32
    tile = (UNIT, LANES)
    gram, *masked = pl.pallas_call(
        functools.partial(gram_kernel, total_rows, ny, nz, nx),
        out_shape=(
            jax.ShapeDtypeStruct((units, *tile), f32),
            *[jax.ShapeDtypeStruct((rows, width), BF16)] * 3,
        ),
        in_specs=[
            pl.BlockSpec(memory_space=pl.ANY),
            pl.BlockSpec(memory_space=pltpu.SMEM),
            pl.BlockSpec(memory_space=pltpu.VMEM),
        ],
        out_specs=(pl.BlockSpec(memory_space=pltpu.VMEM), *[pl.BlockSpec(memory_space=pl.ANY)] * 3),
        scratch_shapes=[
            pltpu.VMEM((rows, width), f32),
            *[pltpu.VMEM((rows, width), BF16)] * 3,
            pltpu.VMEM((units, *tile), f32),
            pltpu.VMEM((n_half, *tile), f32),
            pltpu.VMEM((n_half, *tile), f32),
            pltpu.VMEM((places, n_strip, *tile), f32),
            pltpu.VMEM((n_strip, *tile), f32),
            pltpu.VMEM((nz, n_strip, *tile), f32),
            pltpu.SemaphoreType.DMA((LOADS,)),
            pltpu.SemaphoreType.DMA((3,)),
            pltpu.SemaphoreType.DMA((copies,)),
            pltpu.SemaphoreType.DMA((copies,)),
        ],
        compiler_params=pltpu.CompilerParams(collective_id=0, has_side_effects=True),
        name="gram_allreduce",
    )(snapshots, live_rows, column_order.reshape(1, width))
    return gram.reshape(3 * LANES, LANES), *masked


def pieces(value):
    high = value.astype(BF16)
    rest = value - high.astype(jnp.float32)
    middle = rest.astype(BF16)
    return high, middle, (rest - middle.astype(jnp.float32)).astype(BF16)


def product(a, b, dims):
    out = None
    for p, q in TERMS:
        term = lax.dot_general(a[p], b[q], (dims, ((), ())), preferred_element_type=jnp.float32)
        out = term if out is None else out + term
    return out


def factor_kernel(group, chunk, tail, gram_ref, high_ref, middle_ref, low_ref, basis_ref, tri_ref, pass_ref, work, inverse, right_ref):
    rows, width = high_ref.shape
    blocks = width // TILE
    per_lanes = LANES // TILE
    f32 = jnp.float32
    shape = (TILE, LANES)
    sub = lax.broadcasted_iota(jnp.int32, shape, 0)
    lane = lax.broadcasted_iota(jnp.int32, shape, 1)
    data = (high_ref, middle_ref, low_ref)

    def band(i):
        return slice(i * TILE, (i + 1) * TILE)

    def lanes(v):
        return slice(v * LANES, (v + 1) * LANES)

    work[:LANES, :LANES] = gram_ref[:LANES, :]
    work[:LANES, LANES:] = gram_ref[LANES:2 * LANES, :]
    work[LANES:, :LANES] = jnp.zeros((width - LANES, LANES), f32)
    work[LANES:, LANES:] = gram_ref[2 * LANES:, :]
    row_id = lax.broadcasted_iota(jnp.int32, (width, width), 0)
    col_id = lax.broadcasted_iota(jnp.int32, (width, width), 1)
    identity = (row_id == col_id).astype(f32)
    inverse[...] = identity
    tri_ref[...] = jnp.zeros_like(tri_ref)
    right_ref[0] = identity.astype(BF16)
    right_ref[1] = jnp.zeros((width, width), BF16)
    right_ref[2] = jnp.zeros((width, width), BF16)

    def pass_right():
        left = pieces(inverse[:LOW, :LOW])
        right = pieces(tri_ref[:LOW, :])
        left = jnp.concatenate([left[p] for p, q in TERMS], axis=0)
        right = jnp.concatenate([right[q] for p, q in TERMS], axis=0)
        taken = lax.dot_general(left, right, (((0,), (0,)), ((), ())), preferred_element_type=f32)
        for p, piece in enumerate(pieces(identity[:LOW] - taken)):
            right_ref[p, :LOW, :] = piece

    def finish_pass(c, size):
        here = slice(c * size, (c + 1) * size)
        right = [right_ref[p] for p in range(3)]
        pass_ref[here, :] = product([ref[here, :] for ref in data], right, ((1,), (0,)))

    def finish_basis(c, half, size):
        here = slice(c * size, (c + 1) * size)
        depth = (half + 1) * LANES
        right = [right_ref[p, :LANES, :depth] for p in range(3)]
        basis_ref[here, lanes(half)] = product([ref[here, :depth] for ref in data], right, ((1,), (1,)))

    def basis_right(half):
        depth = (half + 1) * LANES
        for p, piece in enumerate(pieces(inverse[lanes(half), :depth])):
            right_ref[p, :LANES, :depth] = piece

    fillers = []
    pending = None

    for k in range(blocks):
        t = k // per_lanes
        base = (k % per_lanes) * TILE
        s = k // group
        last = min((s + 2) * group, blocks)
        row = {}
        for j in range(TILE):
            r = k * TILE + j
            for v in range(t, width // LANES):
                row["g", v, j] = jnp.broadcast_to(work[r:r + 1, lanes(v)], shape)
            for v in range(0, t + 1):
                row["x", v, j] = jnp.broadcast_to(inverse[r:r + 1, lanes(v)], shape)
        items = [("g", v) for v in range(t, width // LANES)] + [("x", v) for v in range(0, t + 1)]
        a = {}
        for j in range(TILE):
            for m in range(j, TILE):
                a[j, m] = jnp.broadcast_to(row["g", t, j][:, base + m:base + m + 1], shape)
        col = {}
        for i in range(k + 1, last):
            v = i // per_lanes
            if i < (s + 1) * group:
                tile = work[band(i), lanes(v)]
                for j in range(TILE):
                    col[i, j] = jnp.broadcast_to(tile[:, base + j:base + j + 1], shape)
            else:
                here = lane == sub + (i % per_lanes) * TILE
                for j in range(TILE):
                    picked = jnp.where(here, row["g", v, j], 0.0)
                    col[i, j] = jnp.broadcast_to(jnp.sum(picked, axis=1, keepdims=True), shape)
        for j in range(TILE):
            scale = lax.rsqrt(a[j, j])
            for m in range(j + 1, TILE):
                a[j, m] = a[j, m] * scale
            for m in range(j + 1, TILE):
                for p in range(m, TILE):
                    a[m, p] = a[m, p] - a[j, m] * a[j, p]
            for i in range(k + 1, last):
                col[i, j] = col[i, j] * scale
                for m in range(j + 1, TILE):
                    col[i, m] = col[i, m] - a[j, m] * col[i, j]
            for kind, v in items:
                row[kind, v, j] = row[kind, v, j] * scale
                for m in range(j + 1, TILE):
                    row[kind, v, m] = row[kind, v, m] - a[j, m] * row[kind, v, j]
        for i in range(k + 1, last):
            for kind, v in items:
                ref = work if kind == "g" else inverse
                change = [col[i, j] * row[kind, v, j] for j in range(TILE)]
                while len(change) > 1:
                    change = [p + q for p, q in zip(change[::2], change[1::2])]
                ref[band(i), lanes(v)] = ref[band(i), lanes(v)] - change[0]
        for kind, v in items:
            tile = row[kind, v, TILE - 1]
            for j in range(TILE - 2, -1, -1):
                tile = jnp.where(sub == j, row[kind, v, j], tile)
            if kind == "g":
                if v == t:
                    tile = jnp.where(lane >= sub + base, tile, 0.0)
                tri_ref[band(k), lanes(v)] = tile
            else:
                inverse[band(k), lanes(v)] = tile

        if (k + 1) % group == 0:
            if pending is not None:
                at, low, span, drop, fill = pending
                work[at:, low:] = work[at:, low:] - drop
                inverse[at:, :span] = inverse[at:, :span] - fill
                pending = None
            at = (s + 2) * group * TILE
            if at < width:
                done = slice(s * group * TILE, (s + 1) * group * TILE)
                first = (at // LANES) * LANES
                low = first
                span = (t + 1) * LANES
                rest = tri_ref[done, :]
                top = pieces(rest)
                side = pieces(inverse[done, :span])
                left = jnp.concatenate([top[p][:, first:] for p, q in TERMS], axis=0)
                right = jnp.concatenate([top[q][:, low:] for p, q in TERMS], axis=0)
                dims = (((0,), (0,)), ((), ()))
                drop = lax.dot_general(left, right, dims, preferred_element_type=f32)
                right = jnp.concatenate([side[q] for p, q in TERMS], axis=0)
                fill = lax.dot_general(left, right, dims, preferred_element_type=f32)
                pending = at, low, span, drop[at - first:], fill[at - first:]
        if (k + 1) * TILE == LOW:
            fillers.append(pass_right)
            fillers += [functools.partial(finish_pass, c, chunk) for c in range(rows // chunk)]
        if (k + 1) * TILE == LANES:
            fillers.append(functools.partial(basis_right, 0))
            fillers += [functools.partial(finish_basis, c, 0, chunk) for c in range(rows // chunk)]
        if fillers:
            fillers.pop(0)()
    fillers.append(functools.partial(basis_right, 1))
    for c in range(rows // tail):
        fillers.append(functools.partial(finish_basis, c, 1, tail))
    for filler in fillers:
        filler()


def factor_call(gram, high, middle, low, group=2, chunk=128, tail=256):
    rows, width = high.shape
    f32 = jnp.float32
    vmem = pl.BlockSpec(memory_space=pltpu.VMEM)
    square = pltpu.VMEM((width, width), f32)
    return pl.pallas_call(
        functools.partial(factor_kernel, group, chunk, tail),
        out_shape=(
            jax.ShapeDtypeStruct((rows, width), f32),
            jax.ShapeDtypeStruct((width, width), f32),
            jax.ShapeDtypeStruct((rows, width), f32),
        ),
        in_specs=[vmem] * 4,
        out_specs=(vmem, vmem, vmem),
        scratch_shapes=[square, square, pltpu.VMEM((3, width, width), BF16)],
        name="factor",
    )(gram, high, middle, low)


def on_device(sizes, snapshots, live_rows, column_order):
    gram, *masked = masked_and_gram(snapshots, live_rows, column_order, sizes)
    return factor_call(gram, *masked)


def solution(mesh):
    placed = (P(("lon", "lat", "depth"), None), P(("lon", "lat", "depth")), P())
    sizes = (mesh.shape["lon"] // CORES, mesh.shape["lat"], mesh.shape["depth"])
    return jax.shard_map(
        functools.partial(on_device, sizes),
        mesh=mesh,
        in_specs=placed,
        out_specs=(P(("lon", "lat", "depth"), None), P(), P(("lon", "lat", "depth"), None)),
        check_vma=False,
    )
```

time: 50.4 us -> 50 us (level)
    pallas_call x1, Pallas kernels: 11.6 us -> 9.9 us  [factor_call(): pl.pallas_call(functools.partial(factor_kernel, group, chunk, tail), out_...]
    pallas_call x1, Pallas kernels: 37.3 us -> 38.6 us  [masked_and_gram(): pl.pallas_call(functools.partial(gram_kernel, total_rows, ny, nz, nx), ou...]
where the time goes in v4:
time: 50 us; the launch traced here: 49.8 us
  Pallas kernels  48.5 us (97%)
  between operations  1.28 us (3%)
    pallas_call x1, Pallas kernels, masked_and_gram(): pl.pallas_call(functools.partial(gram_kernel, total_rows, ny, nz, nx), ou...  38.6 us
    pallas_call x1, Pallas kernels, factor_call(): pl.pallas_call(functools.partial(factor_kernel, group, chunk, tail), out_...  9.9 us

profile of v4, /device:TPU:1, one launch (start us, length us, event | category | flops | bytes accessed | tf_op | source)
XLA Modules:
  0.0 49.8 jit_solution(3015004978304243747)
XLA Ops:
  1.3 38.6 %gram_allreduce.1 = (f32[96,4,128]{2,1,0:T(4,128)}, bf16[1024,256]{1,0:T(8,128)(2,1)}, bf16[1024,256]{1,0:T(8,128)(2,1)}, bf16[1024,256]{1,0:T(8,128)(2,1)}) custom-call(f32[1024,256]{1,0:T(8,128)} %snap_hbm.1, s32[1]{0:T(128)S(6)} %copy.6.live_ref, s32[1,256]{1,0:T(1,128)} %bitcast.3), custom_call_target="tpu_custom_call" | custom-call | tf_op jit(solution)/shard_map/gram_allreduce/pallas_call | solution.py:157
  39.9 9.9 %factor.1 = (f32[1024,256]{1,0:T(8,128)}, f32[256,256]{1,0:T(8,128)}, f32[1024,256]{1,0:T(8,128)}) custom-call(f32[384,128]{1,0:T(8,128)} %bitcast.2, bf16[1024,256]{1,0:T(8,128)(2,1)} %get-tuple-element.8.high_ref, bf16[1024,256]{1,0:T(8,128)(2,1)} %get-tuple-element.9.middle_ref, bf16[1024,256]{1,0:T(8,128)(2,1)} %get-tuple-element.10.low_ref), custom_call_target="tpu_custom_call" | custom-call | tf_op jit(solution)/shard_map/factor/pallas_call | solution.py:365

commit v5 on v4

--- a/solution.py
+++ b/solution.py
@@ -24,7 +24,7 @@
 
 def gram_kernel(total_rows, ny, nz, nx, snap_hbm, live_ref, order_ref, out_ref, high_hbm, middle_hbm, low_hbm,
                 snap, high_ref, middle_ref, low_ref, gram, from_core, half, from_plane, strip, from_z,
-                load_sem, store_sem, send_sem, recv_sem):
+                load_sem, store_sem, line_sem, send_sem, recv_sem):
     rows, width = snap.shape
     lon = lax.axis_index("lon")
     core, y = lax.rem(lon, CORES), lax.div(lon, CORES)
@@ -58,7 +58,10 @@
         load.start()
         loads.append(load)
 
-    peers = [at_z(d) for d in line] + [at_plane(*d) for d in plane] + [other_core()]
+    reach = -(-nz // 4)
+    near = [d for d in line if hops(d, nz) <= reach]
+    ends = (reach, nz - reach)
+    peers = [at_plane(*d) for d in plane] + [at_z(d) for d in near] + [other_core()]
     barrier = pltpu.get_barrier_semaphore()
     for peer in peers:
         pl.semaphore_signal(barrier, inc=1, device_id=peer, device_id_type=pl.DeviceIdType.MESH)
@@ -89,6 +92,8 @@
         gram[at * per_block:(at + 1) * per_block] = block.reshape(per_block, UNIT, LANES)
 
     pl.semaphore_wait(barrier, len(peers))
+    for d in ends:
+        pl.semaphore_signal(line_sem, inc=1, device_id=at_z(d), device_id_type=pl.DeviceIdType.MESH)
 
     used = [0]
 
@@ -123,6 +128,7 @@
         total = total + from_plane[s]
     strip[...] = total
 
+    pl.semaphore_wait(line_sem, len(ends))
     copies = [send(strip, from_z.at[z], at_z(d)) for d in line]
     from_z[z] = strip[...]
     for copy in copies:
@@ -130,15 +136,21 @@
     total = from_z[0]
     for s in range(1, nz):
         total = total + from_z[s]
-    mine = pl.ds((core * places + place) * n_strip, n_strip)
-    out_ref[mine] = total
-
-    copies = [send(out_ref.at[mine], out_ref.at[mine], at_plane(*d)) for d in plane]
-    for copy in copies:
+
+    def strip_of(p):
+        return out_ref.at[pl.ds((core * places + p) * n_strip, n_strip)]
+
+    out_ref[pl.ds((core * places + place) * n_strip, n_strip)] = total
+    spread = [send(strip_of(place), strip_of(place), at_plane(*d)) for d in plane]
+    handed = [send(strip_of(place), strip_of(place), other_core())]
+    for (dy, dx), copy in zip(reversed(plane), reversed(spread)):
+        copy.wait_recv()
+        source = lax.rem(y + ny - dy, ny) * nx + lax.rem(x + nx - dx, nx)
+        handed.append(send(strip_of(source), strip_of(source), other_core()))
+    for copy in spread:
+        copy.wait_send()
+    for copy in handed:
         copy.wait()
-    mine = pl.ds(core * n_half, n_half)
-    copy = send(out_ref.at[mine], out_ref.at[mine], other_core())
-    copy.wait()
     for store in stores:
         store.wait()
 
@@ -150,7 +162,7 @@
     units = 3 * LANES // UNIT
     n_half = units // CORES
     n_strip = n_half // places
-    copies = 2 + 2 * (places - 1) + (nz - 1)
+    copies = 1 + 2 * (places - 1) + (nz - 1) + places
     total_rows = rows * CORES * places * nz
     f32 = jnp.float32
     tile = (UNIT, LANES)
@@ -177,6 +189,7 @@
             pltpu.VMEM((nz, n_strip, *tile), f32),
             pltpu.SemaphoreType.DMA((LOADS,)),
             pltpu.SemaphoreType.DMA((3,)),
+            pltpu.SemaphoreType.REGULAR,
             pltpu.SemaphoreType.DMA((copies,)),
             pltpu.SemaphoreType.DMA((copies,)),
         ],

time: 50 us -> 49 us (0.980)
  Pallas kernels: 48.5 us -> 47.6 us
    pallas_call x1, Pallas kernels: 38.6 us -> 37.7 us  [masked_and_gram(): pl.pallas_call(functools.partial(gram_kernel, total_rows, ny, nz, nx), ou...]
where the time goes in v5:
time: 49 us; the launch traced here: 48.8 us
  Pallas kernels  47.6 us (97%)
  between operations  1.28 us (3%)
    pallas_call x1, Pallas kernels, masked_and_gram(): pl.pallas_call(functools.partial(gram_kernel, total_rows, ny, nz, nx), ou...  37.7 us
    pallas_call x1, Pallas kernels, factor_call(): pl.pallas_call(functools.partial(factor_kernel, group, chunk, tail), out_...  9.9 us

profile of v5, /device:TPU:1, one launch (start us, length us, event | category | flops | bytes accessed | tf_op | source)
XLA Modules:
  0.0 48.8 jit_solution(8999239344335683038)
XLA Ops:
  1.3 37.7 %gram_allreduce.1 = (f32[96,4,128]{2,1,0:T(4,128)}, bf16[1024,256]{1,0:T(8,128)(2,1)}, bf16[1024,256]{1,0:T(8,128)(2,1)}, bf16[1024,256]{1,0:T(8,128)(2,1)}) custom-call(f32[1024,256]{1,0:T(8,128)} %snap_hbm.1, s32[1]{0:T(128)S(6)} %copy.6.live_ref, s32[1,256]{1,0:T(1,128)} %bitcast.3), custom_call_target="tpu_custom_call" | custom-call | tf_op jit(solution)/shard_map/gram_allreduce/pallas_call | solution.py:169
  38.9 9.9 %factor.1 = (f32[1024,256]{1,0:T(8,128)}, f32[256,256]{1,0:T(8,128)}, f32[1024,256]{1,0:T(8,128)}) custom-call(f32[384,128]{1,0:T(8,128)} %bitcast.2, bf16[1024,256]{1,0:T(8,128)(2,1)} %get-tuple-element.8.high_ref, bf16[1024,256]{1,0:T(8,128)(2,1)} %get-tuple-element.9.middle_ref, bf16[1024,256]{1,0:T(8,128)(2,1)} %get-tuple-element.10.low_ref), custom_call_target="tpu_custom_call" | custom-call | tf_op jit(solution)/shard_map/factor/pallas_call | solution.py:378

commit v6 on v5

--- a/solution.py
+++ b/solution.py
@@ -13,6 +13,7 @@
 TILE = 8
 UNIT = 4
 LOADS = 4
+VMEM_LIMIT = 24 * 2**20
 BF16 = jnp.bfloat16
 TERMS = ((2, 0), (0, 2), (1, 1), (1, 0), (0, 1), (0, 0))
 HIGHEST = lax.Precision.HIGHEST
@@ -22,16 +23,15 @@
     return min(d % n, n - d % n)
 
 
-def gram_kernel(total_rows, ny, nz, nx, snap_hbm, live_ref, order_ref, out_ref, high_hbm, middle_hbm, low_hbm,
-                snap, high_ref, middle_ref, low_ref, gram, from_core, half, from_plane, strip, from_z,
-                load_sem, store_sem, line_sem, send_sem, recv_sem):
+def gram_kernel(total_rows, ny, nz, nx, snap_hbm, live_ref, order_hbm, out_ref, high_ref, middle_ref, low_ref,
+                snap, order_ref, gram, from_core, half, from_plane, strip, from_z,
+                load_sem, small_sem, line_sem, send_sem, recv_sem):
     rows, width = snap.shape
     lon = lax.axis_index("lon")
     core, y = lax.rem(lon, CORES), lax.div(lon, CORES)
     z, x = lax.axis_index("lat"), lax.axis_index("depth")
     f32 = jnp.float32
     data = (high_ref, middle_ref, low_ref)
-    data_hbm = (high_hbm, middle_hbm, low_hbm)
 
     plane = [(dy, dx) for dy in range(ny) for dx in range(nx) if dy or dx]
     plane.sort(key=lambda d: -hops(d[0], ny) - hops(d[1], nx))
@@ -50,6 +50,8 @@
     def at_z(d):
         return {"lat": lax.rem(z + d, nz)}
 
+    picks = pltpu.make_async_copy(order_hbm, order_ref, small_sem)
+    picks.start()
     size = rows // LOADS
     loads = []
     for c in range(LOADS):
@@ -66,6 +68,7 @@
     for peer in peers:
         pl.semaphore_signal(barrier, inc=1, device_id=peer, device_id_type=pl.DeviceIdType.MESH)
 
+    picks.wait()
     select = (lax.broadcasted_iota(jnp.int32, (width, width), 0) == order_ref[...]).astype(BF16)
     for c in range(LOADS):
         loads[c].wait()
@@ -73,12 +76,6 @@
         live = lax.broadcasted_iota(jnp.int32, (size, width), 0) + c * size < live_ref[0]
         for piece, ref in zip(pieces(jnp.where(live, snap[here, :], 0.0)), data):
             ref[here, :] = jnp.dot(piece, select, preferred_element_type=f32).astype(BF16)
-    stores = []
-    for p, (src, dst) in enumerate(zip(data, data_hbm)):
-        store = pltpu.make_async_copy(src, dst, store_sem.at[p])
-        store.start()
-        stores.append(store)
-
     def inner(a, b):
         return lax.dot_general(a, b, (((0,), (0,)), ((), ())), preferred_element_type=f32)
 
@@ -151,8 +148,6 @@
         copy.wait_send()
     for copy in handed:
         copy.wait()
-    for store in stores:
-        store.wait()
 
 
 def masked_and_gram(snapshots, live_rows, column_order, sizes):
@@ -166,6 +161,10 @@
     total_rows = rows * CORES * places * nz
     f32 = jnp.float32
     tile = (UNIT, LANES)
+
+    def in_hbm(array):
+        return pltpu.with_memory_space_constraint(array, pltpu.HBM)
+
     gram, *masked = pl.pallas_call(
         functools.partial(gram_kernel, total_rows, ny, nz, nx),
         out_shape=(
@@ -173,14 +172,14 @@
             *[jax.ShapeDtypeStruct((rows, width), BF16)] * 3,
         ),
         in_specs=[
-            pl.BlockSpec(memory_space=pl.ANY),
+            pl.BlockSpec(memory_space=pltpu.HBM),
             pl.BlockSpec(memory_space=pltpu.SMEM),
-            pl.BlockSpec(memory_space=pltpu.VMEM),
+            pl.BlockSpec(memory_space=pltpu.HBM),
         ],
-        out_specs=(pl.BlockSpec(memory_space=pltpu.VMEM), *[pl.BlockSpec(memory_space=pl.ANY)] * 3),
+        out_specs=(pl.BlockSpec(memory_space=pltpu.VMEM),) * 4,
         scratch_shapes=[
             pltpu.VMEM((rows, width), f32),
-            *[pltpu.VMEM((rows, width), BF16)] * 3,
+            pltpu.VMEM((1, width), jnp.int32),
             pltpu.VMEM((units, *tile), f32),
             pltpu.VMEM((n_half, *tile), f32),
             pltpu.VMEM((n_half, *tile), f32),
@@ -188,14 +187,14 @@
             pltpu.VMEM((n_strip, *tile), f32),
             pltpu.VMEM((nz, n_strip, *tile), f32),
             pltpu.SemaphoreType.DMA((LOADS,)),
-            pltpu.SemaphoreType.DMA((3,)),
+            pltpu.SemaphoreType.DMA,
             pltpu.SemaphoreType.REGULAR,
             pltpu.SemaphoreType.DMA((copies,)),
             pltpu.SemaphoreType.DMA((copies,)),
         ],
-        compiler_params=pltpu.CompilerParams(collective_id=0, has_side_effects=True),
+        compiler_params=pltpu.CompilerParams(collective_id=0, has_side_effects=True, vmem_limit_bytes=VMEM_LIMIT),
         name="gram_allreduce",
-    )(snapshots, live_rows, column_order.reshape(1, width))
+    )(in_hbm(snapshots), live_rows, in_hbm(column_order.reshape(1, width)))
     return gram.reshape(3 * LANES, LANES), *masked
 
 
@@ -385,6 +384,7 @@
         in_specs=[vmem] * 4,
         out_specs=(vmem, vmem, vmem),
         scratch_shapes=[square, square, pltpu.VMEM((3, width, width), BF16)],
+        compiler_params=pltpu.CompilerParams(vmem_limit_bytes=VMEM_LIMIT),
         name="factor",
     )(gram, high, middle, low)
 

time: 49 us -> 46.3 us (0.945)
  Pallas kernels: 47.6 us -> 44.9 us
    pallas_call x1, Pallas kernels: 37.7 us -> 36.2 us  [masked_and_gram(): pl.pallas_call(functools.partial(gram_kernel, total_rows, ny, nz, nx), ou...]
    pallas_call x1, Pallas kernels: 9.9 us -> 8.68 us  [factor_call(): pl.pallas_call(functools.partial(factor_kernel, group, chunk, tail), out_...]
where the time goes in v6:
time: 46.3 us; the launch traced here: 46.2 us
  Pallas kernels  44.9 us (97%)
  between operations  1.28 us (3%)
    pallas_call x1, Pallas kernels, masked_and_gram(): pl.pallas_call(functools.partial(gram_kernel, total_rows, ny, nz, nx), ou...  36.2 us
    pallas_call x1, Pallas kernels, factor_call(): pl.pallas_call(functools.partial(factor_kernel, group, chunk, tail), out_...  8.68 us

profile of v6, /device:TPU:1, one launch (start us, length us, event | category | flops | bytes accessed | tf_op | source)
XLA Modules:
  0.0 46.2 jit_solution(4733959300171635060)
XLA Ops:
  1.3 36.2 %gram_allreduce.1 = (f32[96,4,128]{2,1,0:T(4,128)S(1)}, bf16[1024,256]{1,0:T(8,128)(2,1)S(1)}, bf16[1024,256]{1,0:T(8,128)(2,1)S(1)}, bf16[1024,256]{1,0:T(8,128)(2,1)S(1)}) custom-call(f32[1024,256]{1,0:T(8,128)} %snap_hbm.1, s32[1]{0:T(128)S(6)} %copy.6.live_ref, s32[1,256]{1,0:T(1,128)} %bitcast.3), custom_call_target="tpu_custom_call" | custom-call | tf_op jit(solution)/shard_map/gram_allreduce/pallas_call | solution.py:168
  37.5 8.7 %factor.1 = (f32[1024,256]{1,0:T(8,128)}, f32[256,256]{1,0:T(8,128)}, f32[1024,256]{1,0:T(8,128)}) custom-call(f32[384,128]{1,0:T(8,128)S(1)} %bitcast.2, bf16[1024,256]{1,0:T(8,128)(2,1)S(1)} %get-tuple-element.8.high_ref, bf16[1024,256]{1,0:T(8,128)(2,1)S(1)} %get-tuple-element.9.middle_ref, bf16[1024,256]{1,0:T(8,128)(2,1)S(1)} %get-tuple-element.10.low_ref), custom_call_target="tpu_custom_call" | custom-call | tf_op jit(solution)/shard_map/factor/pallas_call | solution.py:377

commit v7 on v6

--- a/solution.py
+++ b/solution.py
@@ -47,6 +47,10 @@
         ty, tx = in_plane(dy, dx)
         return {"lon": ty * CORES + core, "depth": tx}
 
+    def across(dy, dx):
+        ty, tx = in_plane(dy, dx)
+        return {"lon": ty * CORES + 1 - core, "depth": tx}
+
     def at_z(d):
         return {"lat": lax.rem(z + d, nz)}
 
@@ -63,7 +67,7 @@
     reach = -(-nz // 4)
     near = [d for d in line if hops(d, nz) <= reach]
     ends = (reach, nz - reach)
-    peers = [at_plane(*d) for d in plane] + [at_z(d) for d in near] + [other_core()]
+    peers = [at_plane(*d) for d in plane] + [across(*d) for d in plane] + [at_z(d) for d in near] + [other_core()]
     barrier = pltpu.get_barrier_semaphore()
     for peer in peers:
         pl.semaphore_signal(barrier, inc=1, device_id=peer, device_id_type=pl.DeviceIdType.MESH)
@@ -138,15 +142,12 @@
         return out_ref.at[pl.ds((core * places + p) * n_strip, n_strip)]
 
     out_ref[pl.ds((core * places + place) * n_strip, n_strip)] = total
-    spread = [send(strip_of(place), strip_of(place), at_plane(*d)) for d in plane]
-    handed = [send(strip_of(place), strip_of(place), other_core())]
-    for (dy, dx), copy in zip(reversed(plane), reversed(spread)):
-        copy.wait_recv()
-        source = lax.rem(y + ny - dy, ny) * nx + lax.rem(x + nx - dx, nx)
-        handed.append(send(strip_of(source), strip_of(source), other_core()))
-    for copy in spread:
-        copy.wait_send()
-    for copy in handed:
+    copies = []
+    for d in plane:
+        copies.append(send(strip_of(place), strip_of(place), at_plane(*d)))
+        copies.append(send(strip_of(place), strip_of(place), across(*d)))
+    copies.append(send(strip_of(place), strip_of(place), other_core()))
+    for copy in copies:
         copy.wait()
 
 
@@ -157,7 +158,7 @@
     units = 3 * LANES // UNIT
     n_half = units // CORES
     n_strip = n_half // places
-    copies = 1 + 2 * (places - 1) + (nz - 1) + places
+    copies = 2 + 3 * (places - 1) + (nz - 1)
     total_rows = rows * CORES * places * nz
     f32 = jnp.float32
     tile = (UNIT, LANES)
@@ -369,7 +370,7 @@
         filler()
 
 
-def factor_call(gram, high, middle, low, group=2, chunk=128, tail=256):
+def factor_call(gram, high, middle, low, group=2, chunk=256, tail=256):
     rows, width = high.shape
     f32 = jnp.float32
     vmem = pl.BlockSpec(memory_space=pltpu.VMEM)

time: 46.3 us -> 45.1 us (0.974)
  Pallas kernels: 44.9 us -> 43.7 us
    pallas_call x1, Pallas kernels: 36.2 us -> 35.3 us  [masked_and_gram(): pl.pallas_call(functools.partial(gram_kernel, total_rows, ny, nz, nx), ou...]
where the time goes in v7:
time: 45.1 us; the launch traced here: 45 us
  Pallas kernels  43.7 us (97%)
  between operations  1.28 us (3%)
    pallas_call x1, Pallas kernels, masked_and_gram(): pl.pallas_call(functools.partial(gram_kernel, total_rows, ny, nz, nx), ou...  35.3 us
    pallas_call x1, Pallas kernels, factor_call(): pl.pallas_call(functools.partial(factor_kernel, group, chunk, tail), out_...  8.45 us

profile of v7, /device:TPU:1, one launch (start us, length us, event | category | flops | bytes accessed | tf_op | source)
XLA Modules:
  0.0 45.0 jit_solution(3421770312011202072)
XLA Ops:
  1.3 35.3 %gram_allreduce.1 = (f32[96,4,128]{2,1,0:T(4,128)S(1)}, bf16[1024,256]{1,0:T(8,128)(2,1)S(1)}, bf16[1024,256]{1,0:T(8,128)(2,1)S(1)}, bf16[1024,256]{1,0:T(8,128)(2,1)S(1)}) custom-call(f32[1024,256]{1,0:T(8,128)} %snap_hbm.1, s32[1]{0:T(128)S(6)} %copy.6.live_ref, s32[1,256]{1,0:T(1,128)} %bitcast.3), custom_call_target="tpu_custom_call" | custom-call | tf_op jit(solution)/shard_map/gram_allreduce/pallas_call | solution.py:169
  36.5 8.5 %factor.1 = (f32[1024,256]{1,0:T(8,128)}, f32[256,256]{1,0:T(8,128)}, f32[1024,256]{1,0:T(8,128)}) custom-call(f32[384,128]{1,0:T(8,128)S(1)} %bitcast.2, bf16[1024,256]{1,0:T(8,128)(2,1)S(1)} %get-tuple-element.8.high_ref, bf16[1024,256]{1,0:T(8,128)(2,1)S(1)} %get-tuple-element.9.middle_ref, bf16[1024,256]{1,0:T(8,128)(2,1)S(1)} %get-tuple-element.10.low_ref), custom_call_target="tpu_custom_call" | custom-call | tf_op jit(solution)/shard_map/factor/pallas_call | solution.py:378

commit v8 on v7

--- a/solution.py
+++ b/solution.py
@@ -24,7 +24,7 @@
 
 
 def gram_kernel(total_rows, ny, nz, nx, snap_hbm, live_ref, order_hbm, out_ref, high_ref, middle_ref, low_ref,
-                snap, order_ref, gram, from_core, half, from_plane, strip, from_z,
+                snap, order_ref, gram, from_plane, strip, from_z,
                 load_sem, small_sem, line_sem, send_sem, recv_sem):
     rows, width = snap.shape
     lon = lax.axis_index("lon")
@@ -109,23 +109,26 @@
         return copy
 
     places = ny * nx
-    n_half = half.shape[0]
-    n_strip = n_half // places
+    n_strip = strip.shape[0]
     place = y * nx + x
 
-    copy = send(gram.at[pl.ds((1 - core) * n_half, n_half)], from_core, other_core())
-    copy.wait()
-    half[...] = gram[pl.ds(core * n_half, n_half)] + from_core[...]
+    me = core * places + place
+
+    def part_of(c, p):
+        return pl.ds((c * places + p) * n_strip, n_strip)
 
     copies = []
     for d in plane:
         ty, tx = in_plane(*d)
-        copies.append(send(half.at[pl.ds((ty * nx + tx) * n_strip, n_strip)], from_plane.at[place], at_plane(*d)))
-    from_plane[place] = half[pl.ds(place * n_strip, n_strip)]
+        there = ty * nx + tx
+        copies.append(send(gram.at[part_of(core, there)], from_plane.at[me], at_plane(*d)))
+        copies.append(send(gram.at[part_of(1 - core, there)], from_plane.at[me], across(*d)))
+    copies.append(send(gram.at[part_of(1 - core, place)], from_plane.at[me], other_core()))
+    from_plane[me] = gram[part_of(core, place)]
     for copy in copies:
         copy.wait()
     total = from_plane[0]
-    for s in range(1, places):
+    for s in range(1, CORES * places):
         total = total + from_plane[s]
     strip[...] = total
 
@@ -156,9 +159,8 @@
     ny, nz, nx = sizes
     places = ny * nx
     units = 3 * LANES // UNIT
-    n_half = units // CORES
-    n_strip = n_half // places
-    copies = 2 + 3 * (places - 1) + (nz - 1)
+    n_strip = units // (CORES * places)
+    copies = 2 * (CORES * places - 1) + (nz - 1)
     total_rows = rows * CORES * places * nz
     f32 = jnp.float32
     tile = (UNIT, LANES)
@@ -182,9 +184,7 @@
             pltpu.VMEM((rows, width), f32),
             pltpu.VMEM((1, width), jnp.int32),
             pltpu.VMEM((units, *tile), f32),
-            pltpu.VMEM((n_half, *tile), f32),
-            pltpu.VMEM((n_half, *tile), f32),
-            pltpu.VMEM((places, n_strip, *tile), f32),
+            pltpu.VMEM((CORES * places, n_strip, *tile), f32),
             pltpu.VMEM((n_strip, *tile), f32),
             pltpu.VMEM((nz, n_strip, *tile), f32),
             pltpu.SemaphoreType.DMA((LOADS,)),

time: 45.1 us -> 45.5 us (level)
  no operation moved by 1% of the time
where the time goes in v8:
time: 45.5 us; the launch traced here: 45.3 us
  Pallas kernels  44 us (97%)
  between operations  1.28 us (3%)
    pallas_call x1, Pallas kernels, masked_and_gram(): pl.pallas_call(functools.partial(gram_kernel, total_rows, ny, nz, nx), ou...  35.6 us
    pallas_call x1, Pallas kernels, factor_call(): pl.pallas_call(functools.partial(factor_kernel, group, chunk, tail), out_...  8.46 us

profile of v8, /device:TPU:1, one launch (start us, length us, event | category | flops | bytes accessed | tf_op | source)
XLA Modules:
  0.0 45.3 jit_solution(985316358597994778)
XLA Ops:
  1.3 35.6 %gram_allreduce.1 = (f32[96,4,128]{2,1,0:T(4,128)S(1)}, bf16[1024,256]{1,0:T(8,128)(2,1)S(1)}, bf16[1024,256]{1,0:T(8,128)(2,1)S(1)}, bf16[1024,256]{1,0:T(8,128)(2,1)S(1)}) custom-call(f32[1024,256]{1,0:T(8,128)} %snap_hbm.1, s32[1]{0:T(128)S(6)} %copy.6.live_ref, s32[1,256]{1,0:T(1,128)} %bitcast.3), custom_call_target="tpu_custom_call" | custom-call | tf_op jit(solution)/shard_map/gram_allreduce/pallas_call | solution.py:171
  36.9 8.5 %factor.1 = (f32[1024,256]{1,0:T(8,128)}, f32[256,256]{1,0:T(8,128)}, f32[1024,256]{1,0:T(8,128)}) custom-call(f32[384,128]{1,0:T(8,128)S(1)} %bitcast.2, bf16[1024,256]{1,0:T(8,128)(2,1)S(1)} %get-tuple-element.8.high_ref, bf16[1024,256]{1,0:T(8,128)(2,1)S(1)} %get-tuple-element.9.middle_ref, bf16[1024,256]{1,0:T(8,128)(2,1)S(1)} %get-tuple-element.10.low_ref), custom_call_target="tpu_custom_call" | custom-call | tf_op jit(solution)/shard_map/factor/pallas_call | solution.py:378
